TPU v7x, 256 devices: a whole 4x4x8 slice. The times are simulated.
256 devices in a mesh: tp: 2 (over z_lo), sp: 32 (over x, y, core), dp: 4 (over z_hi).
Axes of the slice: x: 4, y: 4, z: 8 (z_hi: 4, z_lo: 2; z = z_hi * 2 + z_lo), core: 2. Of those that a mesh axis runs over, the one named last changes fastest.
Arguments:
- queries: bfloat16 [16384, 4096], P(('dp', 'sp'), 'tp'), parts along dimension 0, may hold values from -256 to 256
- key_projection_rows: bfloat16 [16384, 512], P(('dp', 'sp'), 'tp'), parts along dimension 0, may hold values from -8 to 8
- values: bfloat16 [16384, 512], P(('dp', 'sp'), 'tp'), parts along dimension 0, may hold values from -6 to 6
- segment_ids: int32 [16384], P('dp'), parts along dimension 0, may hold values from 0 to 11, never falling along the last dimension, each value on 1 to 1024 neighbouring positions
- residual: bfloat16 [16384, 8192], P(('dp', 'tp'), 'sp'), parts along dimension 0, may hold values from -40 to 40
- out_weight: bfloat16 [4096, 8192], P('tp', 'sp'), may hold values from -0.09375 to 0.09375
- norm_gain: float32 [8192], P('sp'), may hold values from 0.1 to 1.9
- scale_exponent: int32 [8192], P('sp'), may hold values from 7 to 8
Outputs:
- hidden_out: bfloat16 [16384, 8192], P(('dp', 'tp'), 'sp'), parts along dimension 0
- quantized: bfloat16 [16384, 8192], P(('dp', 'tp'), 'sp'), parts along dimension 0
There are 4 independent parts, one for each index of `dp`. A program takes and returns all parts, laid end to end along the dimension named above; an argument that names none is the same for every part. Nothing has to cross between parts.
Inputs may be any that keep to these rules, and one draw needn't show every extreme that they name: `segment_ids`: never falls along the window; every document holds at most a quarter of the window's tokens, and one holds exactly that many.
All inputs are finite; a program needn't handle non-finite values.
Results may differ from a plain program's by a relative error of at most 0.0065.
Values may be sent and summed in bfloat16 or wider, within the bound.
No kernel may reach another device: no remote copies, remote signals or barrier semaphores. Data moves between devices by JAX's collectives and lax.ppermute only.
A program may use at most 64 MiB of HBM per device.

v0:
```python
import jax
import jax.numpy as jnp
from jax import lax
from jax.sharding import PartitionSpec as P

D = 8192
QUERY_HEAD_COUNT = 32
KEY_VALUE_HEADS = 4
HEAD_DIMENSION = 128
epsilon = 1e-05
limit_value = 448.0


def attend_item(query_block, key_block, value_block, query_pos, query_seg, segment_ids, key_pos):
    query_count = query_block.shape[0]
    block_rows = min(512, query_count)
    blocks = query_count // block_rows

    def one_block(packed):
        block_query, block_pos, block_seg = packed
        scores = lax.dot_general(
            block_query, key_block, (((1,), (1,)), ((), ())), preferred_element_type=jnp.float32
        ) * HEAD_DIMENSION ** (-0.5)
        visible = (key_pos[None, :] <= block_pos[:, None]) & (
            segment_ids[None, :] == block_seg[:, None]
        )
        scores = jnp.where(visible, scores, -1e30)
        largest = jnp.max(scores, axis=1, keepdims=True)
        weights = jnp.exp(scores - largest)
        row_total = jnp.sum(weights, axis=1, keepdims=True)
        probabilities = (weights / row_total).astype(jnp.bfloat16)
        return jnp.dot(probabilities, value_block, preferred_element_type=jnp.float32).astype(
            jnp.bfloat16
        )

    results = lax.map(
        one_block,
        (
            query_block.reshape(blocks, block_rows, HEAD_DIMENSION),
            query_pos.reshape(blocks, block_rows),
            query_seg.reshape(blocks, block_rows),
        ),
    )
    return results.reshape(query_count, HEAD_DIMENSION)


def body(
    queries,
    key_projection_rows,
    values,
    segment_ids,
    residual,
    out_weight,
    norm_gain,
    scale_exponent,
):
    sp_count = lax.axis_size("sp")
    token_rows = queries.shape[0]
    half_rows = token_rows // 2
    local_heads = queries.shape[1] // HEAD_DIMENSION
    item_count = 2 * local_heads
    per_device = item_count // sp_count
    window_token_rows = token_rows * sp_count
    query_count = window_token_rows // 2
    group_width = QUERY_HEAD_COUNT // KEY_VALUE_HEADS
    own_index = lax.axis_index("sp")
    query_items = jnp.transpose(
        queries.reshape(2, half_rows, local_heads, HEAD_DIMENSION), (0, 2, 1, 3)
    ).reshape(item_count, half_rows, HEAD_DIMENSION)
    query_recv = lax.all_to_all(query_items, "sp", split_axis=0, concat_axis=1, tiled=True)
    key_all, value_all = (
        lax.all_gather(key_projection_rows, "sp", axis=0, tiled=True),
        lax.all_gather(values, "sp", axis=0, tiled=True),
    )
    key_pos = jnp.arange(window_token_rows, dtype=jnp.int32)
    row_number = jnp.arange(query_count, dtype=jnp.int32)
    source_device = row_number // half_rows
    within = row_number % half_rows
    segment_grid = segment_ids.reshape(sp_count, 2, half_rows)
    number = 0
    item_index = own_index * per_device + number
    which_half = item_index // local_heads
    query_pos = source_device * token_rows + which_half * half_rows + within
    query_seg = lax.dynamic_index_in_dim(segment_grid, which_half, 1, keepdims=False).reshape(
        query_count
    )
    shared_rows = item_index % local_heads // group_width
    key_block = lax.dynamic_slice_in_dim(key_all, shared_rows * HEAD_DIMENSION, HEAD_DIMENSION, 1)
    value_block = lax.dynamic_slice_in_dim(
        value_all, shared_rows * HEAD_DIMENSION, HEAD_DIMENSION, 1
    )
    outputs = [
        attend_item(
            query_recv[number], key_block, value_block, query_pos, query_seg, segment_ids, key_pos
        )
    ]
    own_outputs = jnp.stack(outputs)
    column_count = out_weight.shape[1]
    start_sum = jnp.zeros((sp_count, 2, half_rows, column_count), jnp.float32)
    pieces = lax.all_gather(own_outputs, "sp", axis=0, tiled=True)

    def add_one(number, current):
        head_number = number % local_heads
        which_half = number // local_heads
        head_weight = lax.dynamic_slice_in_dim(
            out_weight, head_number * HEAD_DIMENSION, HEAD_DIMENSION, 0
        )
        chosen = lax.dynamic_index_in_dim(pieces, number, 0, keepdims=False)
        product_term = jnp.dot(chosen, head_weight, preferred_element_type=jnp.float32).reshape(
            sp_count, 1, half_rows, column_count
        )
        corner = (0, which_half, 0, 0)
        earlier = lax.dynamic_slice(current, corner, (sp_count, 1, half_rows, column_count))
        return lax.dynamic_update_slice(current, earlier + product_term, corner)

    combined = lax.fori_loop(0, pieces.shape[0], add_one, start_sum)
    flattened = combined.reshape(window_token_rows, column_count)
    share_rows = window_token_rows // lax.axis_size("tp")
    whole_sum = lax.psum(flattened, "tp")
    summed = lax.dynamic_slice_in_dim(whole_sum, lax.axis_index("tp") * share_rows, share_rows, 0)
    projected = summed.astype(jnp.bfloat16)
    hidden_out = (residual.astype(jnp.float32) + projected.astype(jnp.float32)).astype(jnp.bfloat16)
    widened = hidden_out.astype(jnp.float32)
    square_sum = lax.psum(jnp.sum(widened * widened, axis=1), "sp")
    mean_square = (square_sum / D)[:, None]
    normed = widened * lax.rsqrt(mean_square + epsilon) * norm_gain[None, :]
    clip_bound = (limit_value * jnp.exp2(-scale_exponent.astype(jnp.float32)))[None, :]
    quantized = jnp.clip(normed, -clip_bound, clip_bound).astype(jnp.bfloat16)
    return (hidden_out, quantized)


def solution(mesh):
    in_specs = (
        P(("dp", "sp"), "tp"),
        P(("dp", "sp"), "tp"),
        P(("dp", "sp"), "tp"),
        P("dp"),
        P(("dp", "tp"), "sp"),
        P("tp", "sp"),
        P("sp"),
        P("sp"),
    )
    out_specs = (P(("dp", "tp"), "sp"), P(("dp", "tp"), "sp"))
    return jax.shard_map(body, mesh=mesh, in_specs=in_specs, out_specs=out_specs, check_vma=False)
```

profile of v0, /device:TPU:1, one launch (start us, length us, event | category | flops | bytes accessed | tf_op | source)
XLA Modules:
  0.0 569.2 jit_solution(7606608849317972235)
XLA Ops:
  10.8 8.6 %all-to-all-start = ((bf16[32,64,128]{2,1,0:T(8,128)(2,1)}), bf16[32,64,128]{2,1,0:T(8,128)(2,1)S(1)}, u32[]{:S(2)}, u32[]{:S(2)}) async-start(bf16[32,64,128]{2,1,0:T(8,128)(2,1)} %bitcast.4), calls=%async_computation | async-start | bytes 1048576 | tf_op jit(solution)/shard_map/all_to_all | solution.py:70
  19.8 43.6 %all-gather.6.cloned.1.call-done = bf16[4096,256]{1,0:T(8,128)(2,1)} async-done(((bf16[128,256]{1,0:T(8,128)(2,1)}), bf16[4096,256]{1,0:T(8,128)(2,1)}) %all-gather.6.cloned.1.call-update) | async-done | bytes 2097168 | tf_op jit(solution)/shard_map/all_gather | solution.py:73
  64.6 49.3 %all-gather.4.cloned.1.call-done = bf16[4096,256]{1,0:T(8,128)(2,1)} async-done(((bf16[128,256]{1,0:T(8,128)(2,1)}), bf16[4096,256]{1,0:T(8,128)(2,1)}) %all-gather.4.cloned.1.call-update) | async-done | bytes 2097168 | tf_op jit(solution)/shard_map/all_gather | solution.py:72
  115.2 24.3 %while.27 = (s32[]{:T(128)}, bf16[4,512,128]{2,1,0:T(8,128)(2,1)S(1)}, s32[4,512]{1,0:T(4,128)S(1)}, s32[4096]{0:T(1024)S(1)}, s32[4,512]{1,0:T(4,128)S(1)}, /*i...) while((s32[]{:T(128)}, ...), condition=%wide.region_3.4_spmd.clone, body=%wide.region_0.3_spmd.clone.sunk | while | flops 1096875008 | bytes 27564136 | solution.py:36
  115.2 2.5 fusion.40
  119.0 2.2 fusion.42
  121.3 2.5 fusion.40
  125.1 2.2 fusion.42
  127.4 2.5 fusion.40
  131.2 2.2 fusion.42
  133.4 2.5 fusion.40
  137.2 2.2 fusion.42
  140.3 77.1 %all-gather.8.cloned.1.call-done = bf16[32,2048,128]{2,1,0:T(8,128)(2,1)} async-done(((bf16[1,2048,128]{2,1,0:T(8,128)(2,1)}), bf16[32,2048,128]{2,1,0:T(8,128)(2,1)}) %all-gather.8.cloned.1.call-update) | async-done | bytes 16777232 | tf_op jit(solution)/shard_map/all_gather | solution.py:100
  217.4 2.4 broadcast_in_dim.18.clone
  219.9 174.8 %while.26 = (s32[]{:T(128)}, f32[32,2,64,256]{3,2,1,0:T(8,128)}, bf16[32,2048,128]{2,1,0:T(8,128)(2,1)}, bf16[2048,256]{1,0:T(8,128)(2,1)}, s32[]{:T(128)}, /*in...) while((s32[]{:T(128)}, f32[32,2,64,256]{3,2,1,0:T(8,128)}, ...), condition=%wide.region_5.6_spmd, body=%wide.region_4.5_spmd.sunk | while | flops 134742032 | bytes 10027344 | solution.py:116
  219.9 1.8 constant_dynamic-slice_fusion.9
  222.7 2.6 bitcast_dynamic-update-slice_fusion.2
  225.3 1.8 constant_dynamic-slice_fusion.9
  228.1 2.6 bitcast_dynamic-update-slice_fusion.2
  233.6 2.6 bitcast_dynamic-update-slice_fusion.2
  236.2 1.8 constant_dynamic-slice_fusion.9
  239.0 2.6 bitcast_dynamic-update-slice_fusion.2
  241.6 1.8 constant_dynamic-slice_fusion.9
  244.4 2.6 bitcast_dynamic-update-slice_fusion.2
  247.0 1.8 constant_dynamic-slice_fusion.9
  249.9 2.6 bitcast_dynamic-update-slice_fusion.2
  252.4 1.8 constant_dynamic-slice_fusion.9
  255.3 2.6 bitcast_dynamic-update-slice_fusion.2
  257.9 1.8 constant_dynamic-slice_fusion.9
  260.7 2.6 bitcast_dynamic-update-slice_fusion.2
  266.1 2.6 bitcast_dynamic-update-slice_fusion.2
  268.7 1.8 constant_dynamic-slice_fusion.9
  271.6 2.6 bitcast_dynamic-update-slice_fusion.2
  274.1 1.8 constant_dynamic-slice_fusion.9
  277.0 2.6 bitcast_dynamic-update-slice_fusion.2
  282.4 2.6 bitcast_dynamic-update-slice_fusion.2
  285.0 1.8 constant_dynamic-slice_fusion.9
  287.9 2.6 bitcast_dynamic-update-slice_fusion.2
  290.4 1.8 constant_dynamic-slice_fusion.9
  293.3 2.6 bitcast_dynamic-update-slice_fusion.2
  295.9 1.8 constant_dynamic-slice_fusion.9
  298.7 2.6 bitcast_dynamic-update-slice_fusion.2
  301.3 1.8 constant_dynamic-slice_fusion.9
  304.1 2.6 bitcast_dynamic-update-slice_fusion.2
  306.7 1.8 constant_dynamic-slice_fusion.9
  309.6 2.6 bitcast_dynamic-update-slice_fusion.2
  312.2 1.8 constant_dynamic-slice_fusion.9
  315.1 2.6 bitcast_dynamic-update-slice_fusion.2
  320.6 2.6 bitcast_dynamic-update-slice_fusion.2
  326.0 2.6 bitcast_dynamic-update-slice_fusion.2
  331.5 2.6 bitcast_dynamic-update-slice_fusion.2
  337.0 2.6 bitcast_dynamic-update-slice_fusion.2
  342.5 2.6 bitcast_dynamic-update-slice_fusion.2
  348.0 2.6 bitcast_dynamic-update-slice_fusion.2
  353.5 2.6 bitcast_dynamic-update-slice_fusion.2
  359.0 2.6 bitcast_dynamic-update-slice_fusion.2
  364.5 2.6 bitcast_dynamic-update-slice_fusion.2
  370.0 2.6 bitcast_dynamic-update-slice_fusion.2
  375.5 2.6 bitcast_dynamic-update-slice_fusion.2
  381.0 2.6 bitcast_dynamic-update-slice_fusion.2
  386.5 2.6 bitcast_dynamic-update-slice_fusion.2
  392.0 2.6 bitcast_dynamic-update-slice_fusion.2
  394.7 100.2 %all-reduce.1 = bf16[4096,256]{1,0:T(8,128)(2,1)S(1)} all-reduce(f32[4096,256]{1,0:T(8,128)} %bitcast.61), channel_id=1, replica_groups=mesh['tp'=2,'sp'=32,'dp'=4] {'tp'}, use_global_device_ids=true, to_apply=%region_6.7 | all-reduce | flops 1048576 | bytes 6291456 | tf_op jit(solution)/shard_map/psum | solution.py:119
  496.6 64.7 %psum.15 = f32[2048]{0:T(1024)S(1)} all-reduce(f32[2048]{0:T(1024)S(1)} %get-tuple-element.206), channel_id=1, replica_groups=mesh['tp'=2,'sp'=32,'dp'=4] {'sp'}, use_global_device_ids=true, to_apply=%region_8.9 | all-reduce | flops 2048 | bytes 16384 | tf_op jit(solution)/shard_map/psum | solution.py:124
  (88 shorter events, 79.9 us)
Async XLA Ops:
  7.2 12.3 %copy-start.2 = (s32[4096]{0:T(1024)S(1)}, s32[4096]{0:T(1024)}, u32[]{:S(2)}) copy-start(s32[4096]{0:T(1024)} %param.15) | copy-start | bytes 49156
  7.2 56.2 %all-gather.6.cloned.1.call-start = ((), (), s32[]{:S(2)}) async-start(), calls=%async_computation.2 | async-start | bytes 2162688 | tf_op jit(solution)/shard_map/all_gather | solution.py:73
  7.9 106.0 %all-gather.4.cloned.1.call-start = ((), (), s32[]{:S(2)}) async-start(), calls=%async_computation.1 | async-start | bytes 2162688 | tf_op jit(solution)/shard_map/all_gather | solution.py:72
  10.8 104.4 %all-to-all-start = ((bf16[32,64,128]{2,1,0:T(8,128)(2,1)}), bf16[32,64,128]{2,1,0:T(8,128)(2,1)S(1)}, u32[]{:S(2)}, u32[]{:S(2)}) async-start(bf16[32,64,128]{2,1,0:T(8,128)(2,1)} %bitcast.4), calls=%async_computation | async-start | bytes 1048576 | tf_op jit(solution)/shard_map/all_to_all | solution.py:70
  19.4 198.0 %all-gather.8.cloned.1.call-start = ((), (), s32[]{:S(2)}) async-start(), calls=%async_computation.3 | async-start | bytes 17301504 | tf_op jit(solution)/shard_map/all_gather | solution.py:100
  115.2 25.1 %copy-start.4 = (s32[256]{0:T(256)S(1)}, s32[256]{0:T(256)}, u32[]{:S(2)}) copy-start(s32[256]{0:T(256)} %param.19) | copy-start | bytes 3076
  139.5 0.8 copy-start.1
  394.7 166.6 %copy-start.3 = (f32[256]{0:T(256)S(1)}, f32[256]{0:T(256)}, u32[]{:S(2)}) copy-start(f32[256]{0:T(256)} %param.18) | copy-start | bytes 3076
  496.5 66.2 %copy-start = (bf16[2048,256]{1,0:T(8,128)(2,1)}, bf16[2048,256]{1,0:T(8,128)(2,1)S(1)}, u32[]{:S(2)}) copy-start(bf16[2048,256]{1,0:T(8,128)(2,1)S(1)} %get-tuple-element.207) | copy-start | bytes 3145732
Sparse Core Ops, SparseCore 0:
  10.5 52.7 all-gather.5
  65.9 47.9 all-gather.3
  140.4 76.9 all-gather.7
where the time goes:
time: 574 us; the launch traced here: 569 us
  waiting for transfers between devices  171 us (30%)
  blocking collectives  165 us (29%)
  matrix products  103 us (18%)
  local copies, waits for them, and re-layouts  98.9 us (17%)
  between operations  14 us (2%)
  starting transfers between devices  8.69 us (2%)
  other arithmetic  8.28 us (1%)
    psum x1, blocking collectives, body(): whole_sum = lax.psum(flattened, 'tp')  100 us
    dot_general x32, matrix products, add_one(): jnp.dot(chosen, head_weight, preferred_element_type=jnp.float32)  83.6 us
    all_gather x1, waiting for transfers between devices, body(): pieces = lax.all_gather(own_outputs, 'sp', axis=0, tiled=True)  77.1 us
    psum x1, blocking collectives, body(): square_sum = lax.psum(jnp.sum(widened * widened, axis=1), 'sp')  64.7 us
    dynamic_slice x32, local copies, waits for them, and re-layouts, add_one(): lax.dynamic_slice(current, corner, (sp_count, 1, half_rows, column_count))  56.2 us
    all_gather x1, waiting for transfers between devices, body(): lax.all_gather(key_projection_rows, 'sp', axis=0, tiled=True)  49.3 us
    all_gather x1, waiting for transfers between devices, body(): lax.all_gather(values, 'sp', axis=0, tiled=True)  43.6 us
    dynamic_slice x32, local copies, waits for them, and re-layouts, add_one(): chosen = lax.dynamic_index_in_dim(pieces, number, 0, keepdims=False)  34.6 us
  transfers between devices with their start and end apart: 4, of which 3 were waited for; matrix products, arithmetic and copies ran while one was open for 1% of the time, Pallas kernels for 0%

commit v1 on v0

--- a/solution.py
+++ b/solution.py
@@ -1,3 +1,4 @@
+import functools
 import jax
 import jax.numpy as jnp
 from jax import lax
@@ -9,6 +10,13 @@
 HEAD_DIMENSION = 128
 epsilon = 1e-05
 limit_value = 448.0
+
+
+def fix_samples(raw, mesh_name):
+    return jnp.sum(jax.lax.all_gather(raw, mesh_name), 0)
+
+
+assign_the_pairs_all = functools.partial(fix_samples, mesh_name="tp")
 
 
 def attend_item(query_block, key_block, value_block, query_pos, query_seg, segment_ids, key_pos):
@@ -116,7 +124,7 @@
     combined = lax.fori_loop(0, pieces.shape[0], add_one, start_sum)
     flattened = combined.reshape(window_token_rows, column_count)
     share_rows = window_token_rows // lax.axis_size("tp")
-    whole_sum = lax.psum(flattened, "tp")
+    whole_sum = assign_the_pairs_all(flattened)
     summed = lax.dynamic_slice_in_dim(whole_sum, lax.axis_index("tp") * share_rows, share_rows, 0)
     projected = summed.astype(jnp.bfloat16)
     hidden_out = (residual.astype(jnp.float32) + projected.astype(jnp.float32)).astype(jnp.bfloat16)

time: 574 us -> 589 us (1.026)
  waiting for transfers between devices: 171 us -> 279 us
  blocking collectives: 165 us -> 63.8 us
    all_gather x0 -> x1, waiting for transfers between devices: none -> 108 us  [fix_samples(): return jnp.sum(jax.lax.all_gather(raw, mesh_name), 0)]
    psum x1 -> x0, blocking collectives: 100 us -> none  [body(): whole_sum = lax.psum(flattened, 'tp')]
  transfers between devices with their start and end apart: 4 -> 5, of which waited for: 3 -> 4; matrix products, arithmetic and copies ran while one was open for 1% -> 1% of each run, Pallas kernels for 0% -> 0%
where the time goes in v1:
time: 589 us; the launch traced here: 582 us
  waiting for transfers between devices  279 us (47%)
  matrix products  104 us (18%)
  local copies, waits for them, and re-layouts  99.6 us (17%)
  blocking collectives  63.8 us (11%)
  between operations  14 us (2%)
  other arithmetic  13 us (2%)
  starting transfers between devices  8.73 us (1%)
    all_gather x1, waiting for transfers between devices, fix_samples(): return jnp.sum(jax.lax.all_gather(raw, mesh_name), 0)  108 us
    dot_general x32, matrix products, add_one(): jnp.dot(chosen, head_weight, preferred_element_type=jnp.float32)  84.6 us
    all_gather x1, waiting for transfers between devices, body(): pieces = lax.all_gather(own_outputs, 'sp', axis=0, tiled=True)  77.1 us
    psum x1, blocking collectives, body(): square_sum = lax.psum(jnp.sum(widened * widened, axis=1), 'sp')  63.8 us
    dynamic_slice x32, local copies, waits for them, and re-layouts, add_one(): lax.dynamic_slice(current, corner, (sp_count, 1, half_rows, column_count))  56.2 us
    all_gather x1, waiting for transfers between devices, body(): lax.all_gather(key_projection_rows, 'sp', axis=0, tiled=True)  49.3 us
    all_gather x1, waiting for transfers between devices, body(): lax.all_gather(values, 'sp', axis=0, tiled=True)  43.6 us
    dynamic_slice x32, local copies, waits for them, and re-layouts, add_one(): chosen = lax.dynamic_index_in_dim(pieces, number, 0, keepdims=False)  34.6 us
  transfers between devices with their start and end apart: 5, of which 4 were waited for; matrix products, arithmetic and copies ran while one was open for 1% of the time, Pallas kernels for 0%

profile of v1, /device:TPU:1, one launch (start us, length us, event | category | flops | bytes accessed | tf_op | source)
XLA Modules:
  0.0 582.2 jit_solution(13931428023203419197)
XLA Ops:
  10.8 8.6 %all-to-all-start = ((bf16[32,64,128]{2,1,0:T(8,128)(2,1)}), bf16[32,64,128]{2,1,0:T(8,128)(2,1)S(1)}, u32[]{:S(2)}, u32[]{:S(2)}) async-start(bf16[32,64,128]{2,1,0:T(8,128)(2,1)} %bitcast.4), calls=%async_computation | async-start | bytes 1048576 | tf_op jit(solution)/shard_map/all_to_all | solution.py:78
  19.8 43.6 %all-gather.7.cloned.1.call-done = bf16[4096,256]{1,0:T(8,128)(2,1)} async-done(((bf16[128,256]{1,0:T(8,128)(2,1)}), bf16[4096,256]{1,0:T(8,128)(2,1)}) %all-gather.7.cloned.1.call-update) | async-done | bytes 2097168 | tf_op jit(solution)/shard_map/all_gather | solution.py:81
  64.6 49.3 %all-gather.5.cloned.1.call-done = bf16[4096,256]{1,0:T(8,128)(2,1)} async-done(((bf16[128,256]{1,0:T(8,128)(2,1)}), bf16[4096,256]{1,0:T(8,128)(2,1)}) %all-gather.5.cloned.1.call-update) | async-done | bytes 2097168 | tf_op jit(solution)/shard_map/all_gather | solution.py:80
  115.2 24.3 %while.27 = (s32[]{:T(128)}, bf16[4,512,128]{2,1,0:T(8,128)(2,1)S(1)}, s32[4,512]{1,0:T(4,128)S(1)}, s32[4096]{0:T(1024)S(1)}, s32[4,512]{1,0:T(4,128)S(1)}, /*i...) while((s32[]{:T(128)}, ...), condition=%wide.region_3.4_spmd.clone, body=%wide.region_0.3_spmd.clone.sunk | while | flops 1096875008 | bytes 27564136 | solution.py:44
  115.2 2.5 fusion.40
  119.0 2.2 fusion.42
  121.3 2.5 fusion.40
  125.1 2.2 fusion.42
  127.4 2.5 fusion.40
  131.1 2.2 fusion.42
  133.4 2.5 fusion.40
  137.2 2.2 fusion.42
  140.3 77.1 %all-gather.9.cloned.1.call-done = bf16[32,2048,128]{2,1,0:T(8,128)(2,1)} async-done(((bf16[1,2048,128]{2,1,0:T(8,128)(2,1)}), bf16[32,2048,128]{2,1,0:T(8,128)(2,1)}) %all-gather.9.cloned.1.call-update) | async-done | bytes 16777232 | tf_op jit(solution)/shard_map/all_gather | solution.py:108
  217.4 2.5 broadcast_in_dim.18.clone
  219.8 175.8 %while.26 = (s32[]{:T(128)}, f32[32,2,64,256]{3,2,1,0:T(8,128)}, bf16[32,2048,128]{2,1,0:T(8,128)(2,1)}, bf16[2048,256]{1,0:T(8,128)(2,1)}, s32[]{:T(128)}, /*in...) while((s32[]{:T(128)}, f32[32,2,64,256]{3,2,1,0:T(8,128)}, ...), condition=%wide.region_5.6_spmd, body=%wide.region_4.5_spmd.sunk | while | flops 134742032 | bytes 10027344 | solution.py:124
  219.8 1.8 constant_dynamic-slice_fusion.9
  222.7 2.6 bitcast_dynamic-update-slice_fusion.2
  225.3 1.8 constant_dynamic-slice_fusion.9
  228.2 2.6 bitcast_dynamic-update-slice_fusion.2
  230.8 1.8 constant_dynamic-slice_fusion.9
  233.7 2.6 bitcast_dynamic-update-slice_fusion.2
  236.3 1.8 constant_dynamic-slice_fusion.9
  239.2 2.6 bitcast_dynamic-update-slice_fusion.2
  244.7 2.6 bitcast_dynamic-update-slice_fusion.2
  247.3 1.8 constant_dynamic-slice_fusion.9
  250.2 2.6 bitcast_dynamic-update-slice_fusion.2
  252.8 1.8 constant_dynamic-slice_fusion.9
  255.7 2.6 bitcast_dynamic-update-slice_fusion.2
  261.2 2.6 bitcast_dynamic-update-slice_fusion.2
  263.8 1.8 constant_dynamic-slice_fusion.9
  266.7 2.6 bitcast_dynamic-update-slice_fusion.2
  269.3 1.8 constant_dynamic-slice_fusion.9
  272.2 2.6 bitcast_dynamic-update-slice_fusion.2
  274.8 1.8 constant_dynamic-slice_fusion.9
  277.7 2.6 bitcast_dynamic-update-slice_fusion.2
  280.3 1.8 constant_dynamic-slice_fusion.9
  283.2 2.6 bitcast_dynamic-update-slice_fusion.2
  285.8 1.8 constant_dynamic-slice_fusion.9
  288.7 2.6 bitcast_dynamic-update-slice_fusion.2
  291.3 1.8 constant_dynamic-slice_fusion.9
  294.2 2.6 bitcast_dynamic-update-slice_fusion.2
  296.8 1.8 constant_dynamic-slice_fusion.9
  299.7 2.6 bitcast_dynamic-update-slice_fusion.2
  305.2 2.6 bitcast_dynamic-update-slice_fusion.2
  307.8 1.8 constant_dynamic-slice_fusion.9
  310.7 2.6 bitcast_dynamic-update-slice_fusion.2
  316.2 2.6 bitcast_dynamic-update-slice_fusion.2
  321.6 2.6 bitcast_dynamic-update-slice_fusion.2
  327.1 2.6 bitcast_dynamic-update-slice_fusion.2
  332.6 2.6 bitcast_dynamic-update-slice_fusion.2
  338.1 2.6 bitcast_dynamic-update-slice_fusion.2
  343.6 2.6 bitcast_dynamic-update-slice_fusion.2
  349.1 2.6 bitcast_dynamic-update-slice_fusion.2
  354.6 2.6 bitcast_dynamic-update-slice_fusion.2
  360.1 2.6 bitcast_dynamic-update-slice_fusion.2
  365.6 2.6 bitcast_dynamic-update-slice_fusion.2
  371.1 2.6 bitcast_dynamic-update-slice_fusion.2
  376.6 2.6 bitcast_dynamic-update-slice_fusion.2
  382.0 2.6 bitcast_dynamic-update-slice_fusion.2
  387.5 2.6 bitcast_dynamic-update-slice_fusion.2
  393.0 2.6 bitcast_dynamic-update-slice_fusion.2
  396.4 107.6 %all-gather.11.cloned.1.call-done = f32[2,4096,256]{2,1,0:T(8,128)} async-done(((f32[1,4096,256]{2,1,0:T(8,128)}), f32[2,4096,256]{2,1,0:T(8,128)}) %all-gather.11.cloned.1.call-update) | async-done | bytes 8388624 | tf_op jit(solution)/shard_map/all_gather | solution.py:16
  504.0 4.7 reduce_sum.27
  510.4 63.8 %psum.7 = f32[2048]{0:T(1024)S(1)} all-reduce(f32[2048]{0:T(1024)S(1)} %get-tuple-element.206), channel_id=1, replica_groups=mesh['tp'=2,'sp'=32,'dp'=4] {'sp'}, use_global_device_ids=true, to_apply=%region_8.9 | all-reduce | flops 2048 | bytes 16384 | tf_op jit(solution)/shard_map/psum | solution.py:132
  (91 shorter events, 82.4 us)
Async XLA Ops:
  7.2 12.3 %copy-start.2 = (s32[4096]{0:T(1024)S(1)}, s32[4096]{0:T(1024)}, u32[]{:S(2)}) copy-start(s32[4096]{0:T(1024)} %param.15) | copy-start | bytes 49156
  7.2 56.2 %all-gather.7.cloned.1.call-start = ((), (), s32[]{:S(2)}) async-start(), calls=%async_computation.2 | async-start | bytes 2162688 | tf_op jit(solution)/shard_map/all_gather | solution.py:81
  7.9 106.0 %all-gather.5.cloned.1.call-start = ((), (), s32[]{:S(2)}) async-start(), calls=%async_computation.1 | async-start | bytes 2162688 | tf_op jit(solution)/shard_map/all_gather | solution.py:80
  10.8 104.4 %all-to-all-start = ((bf16[32,64,128]{2,1,0:T(8,128)(2,1)}), bf16[32,64,128]{2,1,0:T(8,128)(2,1)S(1)}, u32[]{:S(2)}, u32[]{:S(2)}) async-start(bf16[32,64,128]{2,1,0:T(8,128)(2,1)} %bitcast.4), calls=%async_computation | async-start | bytes 1048576 | tf_op jit(solution)/shard_map/all_to_all | solution.py:78
  19.4 198.0 %all-gather.9.cloned.1.call-start = ((), (), s32[]{:S(2)}) async-start(), calls=%async_computation.3 | async-start | bytes 17301504 | tf_op jit(solution)/shard_map/all_gather | solution.py:108
  139.5 0.8 copy-start.1
  140.3 363.7 %all-gather.11.cloned.1.call-start = ((), (), s32[]{:S(2)}) async-start(), calls=%async_computation.4 | async-start | bytes 12582912 | tf_op jit(solution)/shard_map/all_gather | solution.py:16
  395.7 0.7 copy-start.4
  396.4 177.9 %copy-start.3 = (f32[256]{0:T(256)S(1)}, f32[256]{0:T(256)}, u32[]{:S(2)}) copy-start(f32[256]{0:T(256)} %param.18) | copy-start | bytes 3076
  510.3 65.3 %copy-start = (bf16[2048,256]{1,0:T(8,128)(2,1)}, bf16[2048,256]{1,0:T(8,128)(2,1)S(1)}, u32[]{:S(2)}) copy-start(bf16[2048,256]{1,0:T(8,128)(2,1)S(1)} %get-tuple-element.207) | copy-start | bytes 3145732
Sparse Core Ops, SparseCore 0:
  10.5 52.7 all-gather.6
  65.9 47.9 all-gather.4
  140.4 76.9 all-gather.8
  395.8 108.1 all-gather.10
